TPU v7x, 256 devices: a whole 4x4x8 slice. The times are simulated.
256 devices in a mesh: tm: 16 (over z_lo, x, core), space: 16 (over z_hi, y).
Axes of the slice: x: 4, y: 4, z: 8 (z_hi: 4, z_lo: 2; z = z_hi * 2 + z_lo), core: 2. Of those that a mesh axis runs over, the one named last changes fastest.
Arguments:
- tokens: bfloat16 [1680, 64, 256], P('space', 'tm'), may hold values from -11 to 11
- w_query: bfloat16 [256, 256], replicated, may hold values from -0.375 to 0.375
- w_key: bfloat16 [256, 256], replicated, may hold values from -0.375 to 0.375
- w_value: bfloat16 [256, 256], replicated, may hold values from -0.375 to 0.375
- w_out: bfloat16 [256, 256], replicated, may hold values from -0.375 to 0.375
- mask: int32 [1680, 1680], P('space'), may hold values from 0 to 1, as said below
- decay: float32 [64, 256], P('tm'), may hold values from 0 to 1
- cotangent: float32 [1680, 64, 256], P('space', 'tm'), may hold values from -6 to 6
Outputs:
- grad_tokens: float32 [1680, 64, 256], P('space', 'tm')
- grad_wq: float32 [256, 256], replicated
- grad_wk: float32 [256, 256], replicated
- grad_wv: float32 [256, 256], replicated
- output_weight_gradient: float32 [256, 256], replicated
Inputs may be any that keep to these rules, and one draw needn't show every extreme that they name: `mask`: every token may attend to itself.
All inputs are finite; a program needn't handle non-finite values.
Results may differ from a plain program's by a relative error of at most 0.03.
The roundings to bfloat16 on the way count: a program that leaves them out, or rounds other values in their place, can miss the bound.
Values may be sent and summed in bfloat16 or wider, within the bound.
A program may use at most 128 MiB of HBM per device.

v0:
```python
import math
import jax
import jax.numpy as jnp
from jax import lax
from jax.sharding import PartitionSpec as P

HEADS = 8


def shifted(array, axis, by):
    devices = lax.axis_size(axis)
    pairs = [(i, i + by) for i in range(devices) if 0 <= i + by < devices]
    return lax.ppermute(array, axis, pairs)


def project(rows_flat, weight):
    return jnp.dot(rows_flat, weight, preferred_element_type=jnp.float32).astype(jnp.bfloat16)


def cross(left, right):
    return lax.dot_general(
        left, right, (((0,), (0,)), ((), ())), preferred_element_type=jnp.float32
    )


def back_project(grads_b, weight):
    return lax.dot_general(
        grads_b, weight, (((1,), (1,)), ((), ())), preferred_element_type=jnp.float32
    )


def shards(tokens, w_query, w_key, w_value, w_out, mask, decay, cotangent):
    tok_rows, round_rows, features = tokens.shape
    head_size = features // HEADS
    score_scale = 1.0 / math.sqrt(head_size)
    x_rounds = jnp.swapaxes(tokens, 0, 1)
    flat_rows = x_rounds.reshape(-1, features)
    queries = project(flat_rows, w_query).reshape(round_rows, tok_rows, HEADS, head_size)
    own_keys = project(flat_rows, w_key).reshape(round_rows, tok_rows, features)
    own_values = project(flat_rows, w_value).reshape(round_rows, tok_rows, features)
    all_keys, all_values = (
        lax.all_gather(own_keys, "space", axis=1, tiled=True),
        lax.all_gather(own_values, "space", axis=1, tiled=True),
    )
    random_key_count = all_keys.shape[1]
    all_keys = all_keys.reshape(round_rows, random_key_count, HEADS, head_size)
    all_values = all_values.reshape(round_rows, random_key_count, HEADS, head_size)
    allowed = mask > 0

    def masked_scores(q_round, k_round):
        scores = (
            jnp.einsum("ihe,jhe->hij", q_round, k_round, preferred_element_type=jnp.float32)
            * score_scale
        )
        return jnp.where(allowed[None], scores, -1e30)

    def forward(round_index):
        scores = masked_scores(queries[round_index], all_keys[round_index])
        maxima = jnp.max(scores, axis=2, keepdims=True)
        expons = jnp.exp(scores - maxima)
        totals = jnp.sum(expons, axis=2, keepdims=True)
        probs_b = (expons / totals).astype(jnp.bfloat16)
        stack_result_matrix = jnp.einsum(
            "hij,jhe->ihe", probs_b, all_values[round_index], preferred_element_type=jnp.float32
        )
        return (stack_result_matrix.astype(jnp.bfloat16), maxima, totals)

    attended, maxima, totals = lax.map(forward, jnp.arange(round_rows))
    local_grads = [None] * round_rows
    reach = [None] * round_rows
    local_grads[round_rows - 1] = cotangent[:, round_rows - 1]
    reach[round_rows - 1] = jnp.ones((1, features), jnp.float32)
    for position in range(round_rows - 2, -1, -1):
        local_grads[position] = (
            cotangent[:, position] + decay[position + 1][None] * local_grads[position + 1]
        )
        reach[position] = decay[position + 1][None] * reach[position + 1]
    block_decay = decay[0][None] * reach[0]
    block_update_message = decay[0][None] * local_grads[0]

    def relay(step_index, state):
        incoming, message = state
        incoming = shifted(message.astype(jnp.bfloat16), "tm", -1).astype(message.dtype)
        return (incoming, block_update_message + block_decay * incoming)

    carried, unused = lax.fori_loop(
        0, lax.axis_size("tm"), relay, (jnp.zeros_like(block_update_message), block_update_message)
    )
    grads = jnp.stack(
        [local_grads[position] + reach[position] * carried for position in range(round_rows)],
        axis=0,
    )
    grads_flat = grads.astype(jnp.bfloat16).reshape(-1, features)
    attended_flat = attended.reshape(-1, features)
    output_weight_gradient = cross(attended_flat, grads_flat)
    upstream = (
        back_project(grads_flat, w_out)
        .astype(jnp.bfloat16)
        .reshape(round_rows, tok_rows, HEADS, head_size)
    )
    deltas = jnp.sum(upstream.astype(jnp.float32) * attended.astype(jnp.float32), axis=3)
    deltas = jnp.swapaxes(deltas, 1, 2)[..., None]

    def backward_round(round_index):
        k_round = all_keys[round_index]
        v_round = all_values[round_index]
        q_round = queries[round_index]
        up_round = upstream[round_index]
        scores = masked_scores(q_round, k_round)
        probs = jnp.exp(scores - maxima[round_index]) / totals[round_index]
        slopes = jnp.einsum("ihe,jhe->hij", up_round, v_round, preferred_element_type=jnp.float32)
        score_grads = (probs * (slopes - deltas[round_index])).astype(jnp.bfloat16)
        grad_query = (
            jnp.einsum("hij,jhe->ihe", score_grads, k_round, preferred_element_type=jnp.float32)
            * score_scale
        )
        grad_key = (
            jnp.einsum("hij,ihe->jhe", score_grads, q_round, preferred_element_type=jnp.float32)
            * score_scale
        )
        grad_value = jnp.einsum(
            "hij,ihe->jhe", probs.astype(jnp.bfloat16), up_round, preferred_element_type=jnp.float32
        )
        partials = jnp.concatenate(
            [
                grad_key.reshape(random_key_count, features),
                grad_value.reshape(random_key_count, features),
            ],
            axis=1,
        )
        partials = partials.astype(jnp.bfloat16).astype(jnp.float32)
        return (grad_query.astype(jnp.bfloat16), partials)

    grad_queries, partial_terms = lax.map(backward_round, jnp.arange(round_rows))
    partial_terms = jnp.swapaxes(partial_terms, 0, 1)
    kv_grads = lax.psum_scatter(
        partial_terms.astype(jnp.bfloat16), "space", scatter_dimension=0, tiled=True
    ).astype(jnp.float32)
    kv_grads = jnp.swapaxes(kv_grads, 0, 1)
    grad_keys = kv_grads[..., :features].astype(jnp.bfloat16).reshape(-1, features)
    grad_values = kv_grads[..., features:].astype(jnp.bfloat16).reshape(-1, features)
    grad_q_flat = grad_queries.reshape(-1, features)
    grad_rows = grads.reshape(-1, features) + back_project(grad_q_flat, w_query)
    grad_rows = grad_rows + back_project(grad_keys, w_key) + back_project(grad_values, w_value)
    grad_tokens = jnp.swapaxes(grad_rows.reshape(round_rows, tok_rows, features), 0, 1)
    summed = lax.psum(
        (
            cross(flat_rows, grad_q_flat),
            cross(flat_rows, grad_keys),
            cross(flat_rows, grad_values),
            output_weight_gradient,
        ),
        ("tm", "space"),
    )
    return (grad_tokens, summed[0], summed[1], summed[2], summed[3])


def solution(mesh):
    return jax.shard_map(
        shards,
        mesh=mesh,
        in_specs=(
            P("space", "tm", None),
            P(),
            P(),
            P(),
            P(),
            P("space", None),
            P("tm", None),
            P("space", "tm", None),
        ),
        out_specs=(P("space", "tm", None), P(), P(), P(), P()),
        check_vma=False,
    )
```

profile of v0, /device:TPU:8, one launch (start us, length us, event | category | flops | bytes accessed | tf_op | source)
XLA Modules:
  0.0 1136.6 jit_solution(881701952524546462)
XLA Ops:
  14.5 117.5 %while.38 = (s32[]{:T(128)}, f32[105,256]{1,0:T(8,128)}, bf16[105,256]{1,0:T(8,128)(2,1)S(1)}, f32[1,256]{1,0:T(1,128)S(1)}, f32[105,256]{1,0:T(8,128)S(1)}, /*index=5*/s32[]{:T(128)}) while((s32[]{:T(128)}, f32[105,256]{1,0:T(8,128)}, bf16[105,256]{1,0:T(8,128)(2,1)S(1)}, f32[1,256]{1,0:T(1,128)S(1)}, f32[105,256]{1,0:T(8,128)S(1)}, ...), condition=%wide.region_1.2_spmd, body=%wide.region_0.1_spmd.sunk | while | flops 107522 | bytes 538733 | solution.py:86
  14.5 1.3 collective-permute-start
  15.8 1.8 collective-permute-done
  18.3 1.3 collective-permute-start
  19.6 3.6 collective-permute-done
  23.9 1.3 collective-permute-start
  25.1 4.2 collective-permute-done
  30.0 1.3 collective-permute-start
  31.3 4.6 collective-permute-done
  37.8 4.6 collective-permute-done
  44.4 4.2 collective-permute-done
  50.5 4.2 collective-permute-done
  56.7 4.6 collective-permute-done
  63.2 4.6 collective-permute-done
  69.8 4.6 collective-permute-done
  76.3 5.4 collective-permute-done
  83.7 10.1 collective-permute-done
  95.7 10.1 collective-permute-done
  107.8 7.1 collective-permute-done
  116.8 6.3 collective-permute-done
  125.1 6.3 collective-permute-done
  134.7 6.9 copy.82
  141.5 12.3 %all-gather.5.cloned.1.call-done = bf16[4,1680,256]{2,0,1:T(4,128)(2,1)} async-done(((bf16[4,105,256]{2,0,1:T(4,128)(2,1)}), bf16[4,1680,256]{2,0,1:T(4,128)(2,1)}) %all-gather.5.cloned.1.call-update) | async-done | bytes 3440656 | tf_op jit(solution)/shard_map/all_gather | solution.py:43
  153.8 6.9 copy.85
  160.8 39.1 %while.39 = (s32[]{:T(128)}, bf16[4,105,8,32]{1,3,2,0:T(8,128)(2,1)S(1)}, f32[4,8,105,1]{2,1,3,0:T(8,128)S(1)}, f32[4,8,105,1]{2,1,3,0:T(8,128)S(1)}, s32[4]{0:T...) while((s32[]{:T(128)}, ...), condition=%wide.region_5.6_spmd, body=%wide.region_2.5_spmd.sunk | while | flops 197593216 | bytes 20291880 | solution.py:68
  163.3 2.6 fusion.96
  165.9 1.6 fusion.97
  167.5 3.0 fusion.98
  173.1 2.6 fusion.96
  175.7 1.6 fusion.97
  177.3 3.0 fusion.98
  182.9 2.6 fusion.96
  185.5 1.6 fusion.97
  187.1 3.0 fusion.98
  192.6 2.6 fusion.96
  195.2 1.6 fusion.97
  196.9 3.0 fusion.98
  200.2 316.6 %while.40 = (s32[]{:T(128)}, bf16[4,105,8,32]{1,3,2,0:T(8,128)(2,1)S(1)}, bf16[4,1680,512]{2,0,1:T(4,128)(2,1)}, s32[4]{0:T(128)S(1)}, bf16[4,1680,8,32]{1,3,2,0...) while((s32[]{:T(128)}, ...), condition=%wide.region_8.9_spmd, body=%wide.region_7.8_spmd.sunk | while | flops 467658240 | bytes 43092636 | solution.py:134
  202.8 3.4 exponential_divide_fusion.2
  206.7 2.3 multiply_convert_fusion.2
  209.0 2.3 fusion.109
  212.0 6.3 copy.148
  218.4 61.0 %dynamic_update_slice.29 = bf16[4,1680,512]{2,0,1:T(4,128)(2,1)} dynamic-update-slice(bf16[4,1680,512]{2,0,1:T(4,128)(2,1)} %get-tuple-element.583, bf16[1,1680,512]{2,0,1:T(2,128)(2,1)} %copy.148, s32[]{:T(128)S(6)} %copy.178, s32[]{:T(128)} %constant.35.clone.1..sunk.1, s32[]{:T(128)} %constant.35.clone.1..sunk.1) | dynamic-update-slice | bytes 3440644 | tf_op jit(solution)/shard_map/while/body/jit(dynamic_update_index_in_dim)/dynamic_update_slice | solution.py:134
  281.9 3.4 exponential_divide_fusion.2
  285.9 2.3 multiply_convert_fusion.2
  288.1 2.3 fusion.109
  291.2 6.3 copy.148
  297.5 61.0 %dynamic_update_slice.29 = bf16[4,1680,512]{2,0,1:T(4,128)(2,1)} dynamic-update-slice(bf16[4,1680,512]{2,0,1:T(4,128)(2,1)} %get-tuple-element.583, bf16[1,1680,512]{2,0,1:T(2,128)(2,1)} %copy.148, s32[]{:T(128)S(6)} %copy.178, s32[]{:T(128)} %constant.35.clone.1..sunk.1, s32[]{:T(128)} %constant.35.clone.1..sunk.1) | dynamic-update-slice | bytes 3440644 | tf_op jit(solution)/shard_map/while/body/jit(dynamic_update_index_in_dim)/dynamic_update_slice | solution.py:134
  361.0 3.4 exponential_divide_fusion.2
  365.0 2.3 multiply_convert_fusion.2
  367.3 2.3 fusion.109
  370.3 6.3 copy.148
  376.7 61.0 %dynamic_update_slice.29 = bf16[4,1680,512]{2,0,1:T(4,128)(2,1)} dynamic-update-slice(bf16[4,1680,512]{2,0,1:T(4,128)(2,1)} %get-tuple-element.583, bf16[1,1680,512]{2,0,1:T(2,128)(2,1)} %copy.148, s32[]{:T(128)S(6)} %copy.178, s32[]{:T(128)} %constant.35.clone.1..sunk.1, s32[]{:T(128)} %constant.35.clone.1..sunk.1) | dynamic-update-slice | bytes 3440644 | tf_op jit(solution)/shard_map/while/body/jit(dynamic_update_index_in_dim)/dynamic_update_slice | solution.py:134
  440.2 3.4 exponential_divide_fusion.2
  444.1 2.3 multiply_convert_fusion.2
  446.4 2.3 fusion.109
  449.5 6.3 copy.148
  455.8 61.0 %dynamic_update_slice.29 = bf16[4,1680,512]{2,0,1:T(4,128)(2,1)} dynamic-update-slice(bf16[4,1680,512]{2,0,1:T(4,128)(2,1)} %get-tuple-element.583, bf16[1,1680,512]{2,0,1:T(2,128)(2,1)} %copy.148, s32[]{:T(128)S(6)} %copy.178, s32[]{:T(128)} %constant.35.clone.1..sunk.1, s32[]{:T(128)} %constant.35.clone.1..sunk.1) | dynamic-update-slice | bytes 3440644 | tf_op jit(solution)/shard_map/while/body/jit(dynamic_update_index_in_dim)/dynamic_update_slice | solution.py:134
  522.2 331.0 %all-reduce.5.cloned.1.call-done = bf16[1680,4,512]{2,1,0:T(4,128)(2,1)} async-done(((bf16[1680,4,512]{2,1,0:T(4,128)(2,1)}), bf16[1680,4,512]{2,1,0:T(4,128)(2,1)}) %all-reduce.5.cloned.1.call-update) | async-done | bytes 6881296
  858.3 264.8 %all-reduce.7.cloned.1.call-done = (f32[256,256]{0,1:T(8,128)}, f32[256,256]{0,1:T(8,128)}, f32[256,256]{0,1:T(8,128)}, f32[256,256]{1,0:T(8,128)}) async-done(((f32[256,256]{0,1:T(8,128)}, f32[256,256]{0,1:T(8,128)}, f32[256,256]{0,1:T(8,128)}, f32[256,256]{1,0:T(8,128)}), (f32[256,256]{0,1:T(8,128)}, f32[256,256]{0,1:T(8,128)}, f32[256,256]{0,1:T(8,128)}, ...) | async-done | bytes 1048592 | tf_op jit(solution)/shard_map/psum | solution.py:146
  1123.0 1.8 copy.99
  1124.8 1.8 copy.100
  1126.6 1.8 copy.101
  1128.4 1.7 copy.189
  (162 shorter events, 55.3 us)
Async XLA Ops:
  7.2 5.5 copy-start
  7.2 7.0 copy-start.16
  7.2 126.6 %copy-start.18 = (bf16[256,256]{1,0:T(8,128)(2,1)S(1)}, bf16[256,256]{1,0:T(8,128)(2,1)}, u32[]{:S(2)}) copy-start(bf16[256,256]{1,0:T(8,128)(2,1)} %param.18) | copy-start | bytes 393220
  7.2 127.5 %all-gather.3.cloned.1.call-start = ((), (), s32[]{:S(2)}) async-start(), calls=%async_computation | async-start | bytes 3655680 | tf_op jit(solution)/shard_map/all_gather | solution.py:42
  8.3 125.9 %copy-start.1 = (bf16[420,256]{1,0:T(8,128)(2,1)}, bf16[420,256]{1,0:T(8,128)(2,1)S(1)}, u32[]{:S(2)}) copy-start(bf16[420,256]{1,0:T(8,128)(2,1)S(1)} %reshape.106) | copy-start | bytes 645124
  10.4 124.1 %copy-start.13 = (s32[105,1680]{1,0:T(8,128)S(1)}, s32[105,1680]{1,0:T(8,128)}, u32[]{:S(2)}) copy-start(s32[105,1680]{1,0:T(8,128)} %param.19) | copy-start | bytes 2116804
  10.5 143.4 %all-gather.5.cloned.1.call-start = ((), (), s32[]{:S(2)}) async-start(), calls=%async_computation.1 | async-start | bytes 3655680 | tf_op jit(solution)/shard_map/all_gather | solution.py:43
  12.6 840.6 %all-reduce.5.cloned.1.call-start = ((), (), s32[]{:S(2)}) async-start(), calls=%async_computation.2 | async-start | bytes 13762560
  14.5 3.1 collective-permute-start
  18.3 4.9 collective-permute-start
  23.9 5.5 collective-permute-start
  30.0 5.9 collective-permute-start
  36.5 5.9 collective-permute-start
  43.1 5.5 collective-permute-start
  49.2 5.5 collective-permute-start
  55.4 5.9 collective-permute-start
  61.9 5.9 collective-permute-start
  68.5 5.9 collective-permute-start
  75.0 6.7 collective-permute-start
  82.4 11.3 collective-permute-start
  94.4 11.4 %collective-permute-start = (bf16[105,256]{1,0:T(8,128)(2,1)S(1)}, bf16[105,256]{1,0:T(8,128)(2,1)S(1)}, u32[]{:S(2)}, u32[]{:S(2)}) collective-permute-start(bf16[105,256]{1,0:T(8,128)(2,1)S(1)} %get-tuple-element.520), channel_id=1, source_target_pairs={{16,0},{32,16},{48,32},{64,48},{80,64},{96,80},{112,96},{128,112},... | collective-permute-start | bytes 161288 | tf_op jit(solution)/shard_map/while/body/eval_jaxpr/ppermute | solution.py:13
  106.5 8.4 collective-permute-start
  115.5 7.6 collective-permute-start
  123.8 7.6 collective-permute-start
  133.0 0.7 copy-start.7
  133.0 0.7 copy-start.9
  133.0 0.7 copy-start.11
  133.0 1.4 copy-start.5
  133.8 26.9 %copy-start.3 = (f32[420,256]{1,0:T(8,128)}, f32[420,256]{1,0:T(8,128)S(1)}, u32[]{:S(2)}) copy-start(f32[420,256]{1,0:T(8,128)S(1)} %reshape.105) | copy-start | bytes 1290244
  516.8 0.9 copy-start.6
  516.8 1.0 copy-start.8
  516.8 1.0 copy-start.10
  516.8 1.1 copy-start.12
  516.8 1.2 copy-start.19
  516.8 3.2 copy-start.2
  516.8 5.1 copy-start.4
  516.8 337.7 %copy-start.17 = (bf16[105,4,256]{2,1,0:T(4,128)(2,1)S(1)}, bf16[105,4,256]{2,1,0:T(4,128)(2,1)}, u32[]{:S(2)}) copy-start(bf16[105,4,256]{2,1,0:T(4,128)(2,1)} %param.14) | copy-start | bytes 645124
  516.9 339.8 %copy-start.14 = (bf16[256,256]{1,0:T(8,128)(2,1)S(1)}, bf16[256,256]{1,0:T(8,128)(2,1)}, u32[]{:S(2)}) copy-start(bf16[256,256]{1,0:T(8,128)(2,1)} %param.16) | copy-start | bytes 393220
  516.9 606.2 %all-reduce.7.cloned.1.call-start = ((), (), s32[]{:S(2)}) async-start(), calls=%async_computation.3 | async-start | bytes 2097152 | tf_op jit(solution)/shard_map/psum | solution.py:146
  517.9 339.0 %copy-start.15 = (bf16[256,256]{1,0:T(8,128)(2,1)S(1)}, bf16[256,256]{1,0:T(8,128)(2,1)}, u32[]{:S(2)}) copy-start(bf16[256,256]{1,0:T(8,128)(2,1)} %param.17) | copy-start | bytes 393220
Sparse Core Ops, SparseCore 0:
  11.0 71.6 all-gather.2
  85.7 68.0 all-gather.4
  517.0 336.1 all-reduce.4
  860.4 262.5 all-reduce.6
where the time goes:
time: 1160 us; the launch traced here: 1140 us
  waiting for transfers between devices  694 us (60%)
  local copies, waits for them, and re-layouts  304 us (26%)
  matrix products  66.1 us (6%)
  starting transfers between devices  20.8 us (2%)
  other arithmetic  20 us (2%)
  loops' own time  16.1 us (1%)
  between operations  15 us (1%)
    unnamed x5, waiting for transfers between devices  331 us
    dynamic_update_slice x8, local copies, waits for them, and re-layouts, shards(): lax.map(backward_round, jnp.arange(round_rows))  269 us
    psum x1, waiting for transfers between devices, shards(): lax.psum((cross(flat_rows, grad_q_flat), cross(flat_rows, grad_keys), cro...  265 us
    ppermute x16, waiting for transfers between devices, shifted(): return lax.ppermute(array, axis, pairs)  86.3 us
    dot_general x8, matrix products, masked_scores(): jnp.einsum('ihe,jhe->hij', q_round, k_round, preferred_element_type=jnp.f...  23.9 us
  transfers between devices with their start and end apart: 20, of which 19 were waited for; matrix products, arithmetic and copies ran while one was open for 3% of the time, Pallas kernels for 0%

commit v1 on v0

--- a/solution.py
+++ b/solution.py
@@ -144,13 +144,16 @@
     grad_rows = grad_rows + back_project(grad_keys, w_key) + back_project(grad_values, w_value)
     grad_tokens = jnp.swapaxes(grad_rows.reshape(round_rows, tok_rows, features), 0, 1)
     summed = lax.psum(
-        (
-            cross(flat_rows, grad_q_flat),
-            cross(flat_rows, grad_keys),
-            cross(flat_rows, grad_values),
-            output_weight_gradient,
+        lax.psum(
+            (
+                cross(flat_rows, grad_q_flat),
+                cross(flat_rows, grad_keys),
+                cross(flat_rows, grad_values),
+                output_weight_gradient,
+            ),
+            "space",
         ),
-        ("tm", "space"),
+        "tm",
     )
     return (grad_tokens, summed[0], summed[1], summed[2], summed[3])
 

time: 1160 us -> 1190 us (1.026)
  waiting for transfers between devices: 694 us -> 730 us
    psum x0 -> x1, waiting for transfers between devices: none -> 124 us  [shards(): lax.psum(lax.psum((cross(flat_rows, grad_q_flat), cross(flat_rows, grad_k...]
    psum x1, waiting for transfers between devices: 265 us -> 175 us  [shards(): lax.psum((cross(flat_rows, grad_q_flat), cross(flat_rows, grad_keys), cro...]
    unnamed x5 -> x6, waiting for transfers between devices: 331 us -> 332 us
  transfers between devices with their start and end apart: 20 -> 21, of which waited for: 19 -> 20; matrix products, arithmetic and copies ran while one was open for 3% -> 2% of each run, Pallas kernels for 0% -> 0%
where the time goes in v1:
time: 1190 us; the launch traced here: 1170 us
  waiting for transfers between devices  730 us (61%)
  local copies, waits for them, and re-layouts  304 us (26%)
  matrix products  66.4 us (6%)
  starting transfers between devices  20.9 us (2%)
  other arithmetic  20.2 us (2%)
  loops' own time  16.1 us (1%)
  between operations  15 us (1%)
    unnamed x6, waiting for transfers between devices  332 us
    dynamic_update_slice x8, local copies, waits for them, and re-layouts, shards(): lax.map(backward_round, jnp.arange(round_rows))  269 us
    psum x1, waiting for transfers between devices, shards(): lax.psum((cross(flat_rows, grad_q_flat), cross(flat_rows, grad_keys), cro...  175 us
    psum x1, waiting for transfers between devices, shards(): lax.psum(lax.psum((cross(flat_rows, grad_q_flat), cross(flat_rows, grad_k...  124 us
    ppermute x16, waiting for transfers between devices, shifted(): return lax.ppermute(array, axis, pairs)  86.3 us
    dot_general x8, matrix products, masked_scores(): jnp.einsum('ihe,jhe->hij', q_round, k_round, preferred_element_type=jnp.f...  23.9 us
  transfers between devices with their start and end apart: 21, of which 20 were waited for; matrix products, arithmetic and copies ran while one was open for 2% of the time, Pallas kernels for 0%

profile of v1, /device:TPU:8, one launch (start us, length us, event | category | flops | bytes accessed | tf_op | source)
XLA Modules:
  0.0 1172.0 jit_solution(16082452209460414612)
XLA Ops:
  14.5 117.6 %while.38 = (s32[]{:T(128)}, f32[105,256]{1,0:T(8,128)}, bf16[105,256]{1,0:T(8,128)(2,1)S(1)}, f32[1,256]{1,0:T(1,128)S(1)}, f32[105,256]{1,0:T(8,128)S(1)}, /*index=5*/s32[]{:T(128)}) while((s32[]{:T(128)}, f32[105,256]{1,0:T(8,128)}, bf16[105,256]{1,0:T(8,128)(2,1)S(1)}, f32[1,256]{1,0:T(1,128)S(1)}, f32[105,256]{1,0:T(8,128)S(1)}, ...), condition=%wide.region_1.2_spmd, body=%wide.region_0.1_spmd.sunk | while | flops 107522 | bytes 538733 | solution.py:86
  14.5 1.3 collective-permute-start
  15.8 1.8 collective-permute-done
  18.3 1.3 collective-permute-start
  19.6 3.6 collective-permute-done
  23.9 1.3 collective-permute-start
  25.1 4.2 collective-permute-done
  31.3 4.6 collective-permute-done
  37.8 4.6 collective-permute-done
  44.4 4.2 collective-permute-done
  50.5 4.2 collective-permute-done
  56.7 4.6 collective-permute-done
  63.2 4.6 collective-permute-done
  69.8 4.6 collective-permute-done
  76.3 5.4 collective-permute-done
  83.7 10.0 collective-permute-done
  95.7 10.1 collective-permute-done
  107.8 7.1 collective-permute-done
  116.9 6.2 collective-permute-done
  125.0 6.4 collective-permute-done
  134.7 6.9 copy.82
  141.7 12.1 %all-gather.5.cloned.1.call-done = bf16[4,1680,256]{2,0,1:T(4,128)(2,1)} async-done(((bf16[4,105,256]{2,0,1:T(4,128)(2,1)}), bf16[4,1680,256]{2,0,1:T(4,128)(2,1)}) %all-gather.5.cloned.1.call-update) | async-done | bytes 3440656 | tf_op jit(solution)/shard_map/all_gather | solution.py:43
  153.8 6.8 copy.85
  160.7 39.7 %while.39 = (s32[]{:T(128)}, bf16[4,105,8,32]{1,3,2,0:T(8,128)(2,1)S(1)}, f32[4,8,105,1]{2,1,3,0:T(8,128)S(1)}, f32[4,8,105,1]{2,1,3,0:T(8,128)S(1)}, s32[4]{0:T...) while((s32[]{:T(128)}, ...), condition=%wide.region_5.6_spmd, body=%wide.region_2.5_spmd.sunk | while | flops 197593216 | bytes 20291880 | solution.py:68
  163.2 2.6 fusion.96
  165.8 1.7 fusion.97
  167.5 3.1 fusion.98
  173.1 2.6 fusion.96
  175.7 1.7 fusion.97
  177.4 3.1 fusion.98
  183.0 2.6 fusion.96
  185.6 1.7 fusion.97
  187.3 3.1 fusion.98
  193.0 2.6 fusion.96
  195.6 1.7 fusion.97
  197.2 3.1 fusion.98
  200.7 316.2 %while.40 = (s32[]{:T(128)}, bf16[4,105,8,32]{1,3,2,0:T(8,128)(2,1)S(1)}, bf16[4,1680,512]{2,0,1:T(4,128)(2,1)}, s32[4]{0:T(128)S(1)}, bf16[4,1680,8,32]{1,3,2,0...) while((s32[]{:T(128)}, ...), condition=%wide.region_8.9_spmd, body=%wide.region_7.8_spmd.sunk | while | flops 467658240 | bytes 43092636 | solution.py:134
  203.3 3.4 exponential_divide_fusion.2
  207.2 2.2 multiply_convert_fusion.2
  209.4 2.3 fusion.109
  212.5 6.3 copy.148
  218.8 60.9 %dynamic_update_slice.29 = bf16[4,1680,512]{2,0,1:T(4,128)(2,1)} dynamic-update-slice(bf16[4,1680,512]{2,0,1:T(4,128)(2,1)} %get-tuple-element.587, bf16[1,1680,512]{2,0,1:T(2,128)(2,1)} %copy.148, s32[]{:T(128)S(6)} %copy.178, s32[]{:T(128)} %constant.35.clone.1..sunk.1, s32[]{:T(128)} %constant.35.clone.1..sunk.1) | dynamic-update-slice | bytes 3440644 | tf_op jit(solution)/shard_map/while/body/jit(dynamic_update_index_in_dim)/dynamic_update_slice | solution.py:134
  282.3 3.4 exponential_divide_fusion.2
  286.3 2.2 multiply_convert_fusion.2
  288.5 2.3 fusion.109
  291.6 6.3 copy.148
  297.9 60.9 %dynamic_update_slice.29 = bf16[4,1680,512]{2,0,1:T(4,128)(2,1)} dynamic-update-slice(bf16[4,1680,512]{2,0,1:T(4,128)(2,1)} %get-tuple-element.587, bf16[1,1680,512]{2,0,1:T(2,128)(2,1)} %copy.148, s32[]{:T(128)S(6)} %copy.178, s32[]{:T(128)} %constant.35.clone.1..sunk.1, s32[]{:T(128)} %constant.35.clone.1..sunk.1) | dynamic-update-slice | bytes 3440644 | tf_op jit(solution)/shard_map/while/body/jit(dynamic_update_index_in_dim)/dynamic_update_slice | solution.py:134
  361.4 3.4 exponential_divide_fusion.2
  365.3 2.2 multiply_convert_fusion.2
  367.5 2.3 fusion.109
  370.6 6.3 copy.148
  376.9 60.9 %dynamic_update_slice.29 = bf16[4,1680,512]{2,0,1:T(4,128)(2,1)} dynamic-update-slice(bf16[4,1680,512]{2,0,1:T(4,128)(2,1)} %get-tuple-element.587, bf16[1,1680,512]{2,0,1:T(2,128)(2,1)} %copy.148, s32[]{:T(128)S(6)} %copy.178, s32[]{:T(128)} %constant.35.clone.1..sunk.1, s32[]{:T(128)} %constant.35.clone.1..sunk.1) | dynamic-update-slice | bytes 3440644 | tf_op jit(solution)/shard_map/while/body/jit(dynamic_update_index_in_dim)/dynamic_update_slice | solution.py:134
  440.4 3.4 exponential_divide_fusion.2
  444.4 2.2 multiply_convert_fusion.2
  446.6 2.3 fusion.109
  449.7 6.3 copy.148
  456.0 60.9 %dynamic_update_slice.29 = bf16[4,1680,512]{2,0,1:T(4,128)(2,1)} dynamic-update-slice(bf16[4,1680,512]{2,0,1:T(4,128)(2,1)} %get-tuple-element.587, bf16[1,1680,512]{2,0,1:T(2,128)(2,1)} %copy.148, s32[]{:T(128)S(6)} %copy.178, s32[]{:T(128)} %constant.35.clone.1..sunk.1, s32[]{:T(128)} %constant.35.clone.1..sunk.1) | dynamic-update-slice | bytes 3440644 | tf_op jit(solution)/shard_map/while/body/jit(dynamic_update_index_in_dim)/dynamic_update_slice | solution.py:134
  522.0 332.0 %all-reduce.7.cloned.1.call-done = bf16[1680,4,512]{2,1,0:T(4,128)(2,1)} async-done(((bf16[1680,4,512]{2,1,0:T(4,128)(2,1)}), bf16[1680,4,512]{2,1,0:T(4,128)(2,1)}) %all-reduce.7.cloned.1.call-update) | async-done | bytes 6881296
  857.4 174.9 %all-reduce.9.cloned.1.call-done = (f32[256,256]{0,1:T(8,128)}, f32[256,256]{0,1:T(8,128)}, f32[256,256]{0,1:T(8,128)}, f32[256,256]{1,0:T(8,128)}) async-done(((f32[256,256]{0,1:T(8,128)}, f32[256,256]{0,1:T(8,128)}, f32[256,256]{0,1:T(8,128)}, f32[256,256]{1,0:T(8,128)}), (f32[256,256]{0,1:T(8,128)}, f32[256,256]{0,1:T(8,128)}, f32[256,256]{0,1:T(8,128)}, ...) | async-done | bytes 1048592 | tf_op jit(solution)/shard_map/psum | solution.py:147
  1034.4 124.0 %all-reduce.11.cloned.1.call-done = (f32[256,256]{0,1:T(8,128)}, f32[256,256]{0,1:T(8,128)}, f32[256,256]{0,1:T(8,128)}, f32[256,256]{1,0:T(8,128)}) async-done(((f32[256,256]{0,1:T(8,128)}, f32[256,256]{0,1:T(8,128)}, f32[256,256]{0,1:T(8,128)}, f32[256,256]{1,0:T(8,128)}), (f32[256,256]{0,1:T(8,128)}, f32[256,256]{0,1:T(8,128)}, f32[256,256]{0,1:T(8,128)}, ...) | async-done | bytes 1048592 | tf_op jit(solution)/shard_map/psum | solution.py:146
  1158.4 1.8 copy.99
  1160.2 1.8 copy.100
  1162.0 1.8 copy.101
  1163.8 1.7 copy.193
  (165 shorter events, 56.7 us)
Async XLA Ops:
  7.2 5.5 copy-start
  7.2 7.0 copy-start.16
  7.2 126.7 %copy-start.18 = (bf16[256,256]{1,0:T(8,128)(2,1)S(1)}, bf16[256,256]{1,0:T(8,128)(2,1)}, u32[]{:S(2)}) copy-start(bf16[256,256]{1,0:T(8,128)(2,1)} %param.18) | copy-start | bytes 393220
  7.2 127.5 %all-gather.3.cloned.1.call-start = ((), (), s32[]{:S(2)}) async-start(), calls=%async_computation | async-start | bytes 3655680 | tf_op jit(solution)/shard_map/all_gather | solution.py:42
  8.3 126.0 %copy-start.1 = (bf16[420,256]{1,0:T(8,128)(2,1)}, bf16[420,256]{1,0:T(8,128)(2,1)S(1)}, u32[]{:S(2)}) copy-start(bf16[420,256]{1,0:T(8,128)(2,1)S(1)} %reshape.106) | copy-start | bytes 645124
  10.4 124.2 %copy-start.13 = (s32[105,1680]{1,0:T(8,128)S(1)}, s32[105,1680]{1,0:T(8,128)}, u32[]{:S(2)}) copy-start(s32[105,1680]{1,0:T(8,128)} %param.19) | copy-start | bytes 2116804
  10.5 143.3 %all-gather.5.cloned.1.call-start = ((), (), s32[]{:S(2)}) async-start(), calls=%async_computation.1 | async-start | bytes 3655680 | tf_op jit(solution)/shard_map/all_gather | solution.py:43
  12.6 841.5 %all-reduce.7.cloned.1.call-start = ((), (), s32[]{:S(2)}) async-start(), calls=%async_computation.2 | async-start | bytes 13762560
  14.5 3.1 collective-permute-start
  18.3 4.9 collective-permute-start
  23.9 5.5 collective-permute-start
  30.0 5.9 collective-permute-start
  36.5 5.9 collective-permute-start
  43.1 5.5 collective-permute-start
  49.2 5.5 collective-permute-start
  55.4 5.9 collective-permute-start
  61.9 5.9 collective-permute-start
  68.5 5.9 collective-permute-start
  75.0 6.7 collective-permute-start
  82.4 11.3 collective-permute-start
  94.4 11.4 collective-permute-start
  106.5 8.4 collective-permute-start
  115.6 7.5 collective-permute-start
  123.8 7.7 collective-permute-start
  133.1 0.6 copy-start.5
  133.1 0.7 copy-start.7
  133.1 0.7 copy-start.9
  133.1 0.8 copy-start.11
  133.9 26.7 %copy-start.3 = (f32[420,256]{1,0:T(8,128)}, f32[420,256]{1,0:T(8,128)S(1)}, u32[]{:S(2)}) copy-start(f32[420,256]{1,0:T(8,128)S(1)} %reshape.105) | copy-start | bytes 1290244
  516.9 0.9 copy-start.6
  516.9 1.0 copy-start.8
  516.9 1.0 copy-start.10
  516.9 1.1 copy-start.12
  516.9 1.2 copy-start.19
  516.9 3.3 copy-start.2
  516.9 338.4 %copy-start.17 = (bf16[105,4,256]{2,1,0:T(4,128)(2,1)S(1)}, bf16[105,4,256]{2,1,0:T(4,128)(2,1)}, u32[]{:S(2)}) copy-start(bf16[105,4,256]{2,1,0:T(4,128)(2,1)} %param.14) | copy-start | bytes 645124
  517.0 515.3 %copy-start.4 = (f32[420,256]{1,0:T(8,128)S(1)}, f32[420,256]{1,0:T(8,128)}, u32[]{:S(2)}) copy-start(f32[420,256]{1,0:T(8,128)} %copy-done.3) | copy-start | bytes 1290244
  517.0 515.3 %all-reduce.9.cloned.1.call-start = ((), (), s32[]{:S(2)}) async-start(), calls=%async_computation.3 | async-start | bytes 2097152 | tf_op jit(solution)/shard_map/psum | solution.py:147
  518.0 514.8 %copy-start.14 = (bf16[256,256]{1,0:T(8,128)(2,1)S(1)}, bf16[256,256]{1,0:T(8,128)(2,1)}, u32[]{:S(2)}) copy-start(bf16[256,256]{1,0:T(8,128)(2,1)} %param.16) | copy-start | bytes 393220
  519.5 513.5 %copy-start.15 = (bf16[256,256]{1,0:T(8,128)(2,1)S(1)}, bf16[256,256]{1,0:T(8,128)(2,1)}, u32[]{:S(2)}) copy-start(bf16[256,256]{1,0:T(8,128)(2,1)} %param.17) | copy-start | bytes 393220
  857.3 301.1 %all-reduce.11.cloned.1.call-start = ((), (), s32[]{:S(2)}) async-start(), calls=%async_computation.4 | async-start | bytes 2097152 | tf_op jit(solution)/shard_map/psum | solution.py:146
Sparse Core Ops, SparseCore 0:
  11.0 71.6 all-gather.2
  85.8 67.9 all-gather.4
  517.1 336.9 all-reduce.6
  857.6 174.6 all-reduce.8
  1035.0 123.4 all-reduce.10
